TPU v7x, 32 devices: a whole 2x2x4 slice. The times are simulated.
32 devices in a mesh: ctx: 4 (over z), tp: 8 (over y, x, core).
Axes of the slice: x: 2, y: 2, z: 4, core: 2. Of those that a mesh axis runs over, the one named last changes fastest.
Arguments:
- token_ids: int32 [2048], P('ctx'), may hold values from 0 to 200063
- marks: int32 [2048], P('ctx'), may hold values 0 or 1
- table: bfloat16 [256, 3072], P(None, 'tp'), may hold values from -6 to 6
- norm_gain: bfloat16 [3072], replicated, may hold values from 0.099609375 to 1.8984375
- w_query: bfloat16 [3072, 4096], P(None, 'tp'), may hold values from -0.109375 to 0.109375
- w_key: bfloat16 [3072, 4096], P(None, 'tp'), may hold values from -0.109375 to 0.109375
- w_value: bfloat16 [3072, 4096], P(None, 'tp'), may hold values from -0.109375 to 0.109375
- decay_idx: int32 [32], P('tp'), may hold values from 21 to 84
- out_gain: bfloat16 [4096], P('tp'), may hold values from 0.099609375 to 1.8984375
- w_out: bfloat16 [4096, 3072], P('tp'), may hold values from -0.125 to 0.125
Outputs:
- mixed: bfloat16 [2048, 3072], P('ctx', 'tp')
All inputs are finite; a program needn't handle non-finite values. No bound on the sum of `marks` on one device may be relied on, other than what follows from the above.
Results may differ from a plain program's by a relative error of at most 0.014.
Values may be sent and summed in bfloat16 or wider, within the bound.
A program may use at most 128 MiB of HBM per device.

v0:
```python
import math

import jax
import jax.numpy as jnp
from jax import lax
from jax.sharding import PartitionSpec as P

mark_keep = 0.75


def entering(x, axis, combine, identity):
    count, place = (lax.axis_size(axis), lax.axis_index(axis))
    everything = jax.tree.map(
        lambda part, kind: lax.all_gather(part.astype(kind), axis), x, (jnp.bfloat16, jnp.bfloat16)
    )
    start = jax.tree.map(
        lambda part, zero: jnp.broadcast_to(jnp.asarray(zero, part.dtype), part.shape), x, identity
    )

    def hop(k, before):
        reached = k < place
        new = combine(
            before, jax.tree.map(lambda part, own: part[k].astype(own.dtype), everything, x)
        )
        return jax.tree.map(lambda a, b: jnp.where(reached, a, b), new, before)

    return lax.fori_loop(0, count, hop, start)


def combine_states(earlier, later):
    return (later[0] + jnp.exp(later[1])[:, None, None] * earlier[0], earlier[1] + later[1])


def per_device(
    token_ids, marks, table, norm_gain, w_query, w_key, w_value, decay_idx, out_gain, w_out
):
    buckets = table.shape[0]
    row_count = token_ids.shape[0]
    head_count = decay_idx.shape[0]
    head_width = w_query.shape[1] // head_count
    hashed = (token_ids * 7919 + 13) % buckets
    one_hot = (hashed[:, None] == jnp.arange(buckets, dtype=jnp.int32)[None, :]).astype(
        jnp.bfloat16
    )
    local_x = jnp.dot(one_hot, table, preferred_element_type=jnp.float32).astype(jnp.bfloat16)
    full_x = lax.all_gather(local_x, "tp", axis=1, tiled=True)
    x_float = full_x.astype(jnp.float32)
    inv_rms = lax.rsqrt(jnp.mean(x_float * x_float, axis=1, keepdims=True) + 1e-05)
    normed = (x_float * inv_rms * norm_gain.astype(jnp.float32)).astype(jnp.bfloat16)
    query_rows = (
        jax.nn.silu(jnp.dot(normed, w_query, preferred_element_type=jnp.float32))
        .astype(jnp.bfloat16)
        .reshape(row_count, head_count, head_width)
    )
    key_rows = (
        jax.nn.silu(jnp.dot(normed, w_key, preferred_element_type=jnp.float32))
        .astype(jnp.bfloat16)
        .reshape(row_count, head_count, head_width)
    )
    value_rows = (
        jnp.dot(normed, w_value, preferred_element_type=jnp.float32)
        .astype(jnp.bfloat16)
        .reshape(row_count, head_count, head_width)
    )
    base_rate = -jnp.exp2(-0.25 * decay_idx.astype(jnp.float32))
    log_decay = base_rate[None, :] + marks.astype(jnp.float32)[:, None] * math.log(mark_keep)
    cumulative = jnp.cumsum(log_decay, axis=0)
    per_head = cumulative.T
    gaps_log = per_head[:, :, None] - per_head[:, None, :]
    causal = jnp.arange(row_count)[:, None] >= jnp.arange(row_count)[None, :]
    decay_mask = jnp.where(causal[None], jnp.exp(jnp.minimum(gaps_log, 0.0)), 0.0)
    scores = jnp.einsum("thd,shd->hts", query_rows, key_rows, preferred_element_type=jnp.float32)
    weights = (scores * decay_mask).astype(jnp.bfloat16)
    intra_part = jnp.einsum("hts,shd->thd", weights, value_rows, preferred_element_type=jnp.float32)
    block_decay = cumulative[-1]
    decayed = (
        key_rows.astype(jnp.float32) * jnp.exp(block_decay[None, :] - cumulative)[:, :, None]
    ).astype(jnp.bfloat16)
    local_state = jnp.einsum(
        "shd,she->hde", decayed, value_rows, preferred_element_type=jnp.float32
    )
    empty_state = jnp.zeros_like(local_state)
    incoming, _ = entering(
        (local_state, block_decay),
        "ctx",
        combine_states,
        (empty_state, jnp.zeros_like(block_decay)),
    )
    carried = jnp.einsum(
        "thd,hde->the", query_rows.astype(jnp.float32), incoming, precision=lax.Precision.HIGHEST
    )
    attended = intra_part + jnp.exp(cumulative)[:, :, None] * carried
    out_scale = lax.rsqrt(jnp.mean(attended * attended, axis=2, keepdims=True) + 1e-06)
    normal_out = (
        attended * out_scale * out_gain.astype(jnp.float32).reshape(head_count, head_width)
    ).astype(jnp.bfloat16)
    partial_value = jnp.dot(
        normal_out.reshape(row_count, head_count * head_width),
        w_out,
        preferred_element_type=jnp.float32,
    )
    summed = lax.psum_scatter(
        partial_value.astype(jnp.bfloat16), "tp", scatter_dimension=1, tiled=True
    ).astype(jnp.float32)
    return (local_x.astype(jnp.float32) + summed).astype(jnp.bfloat16)


def solution(mesh):
    return jax.shard_map(
        per_device,
        mesh=mesh,
        in_specs=(
            P("ctx"),
            P("ctx"),
            P(None, "tp"),
            P(),
            P(None, "tp"),
            P(None, "tp"),
            P(None, "tp"),
            P("tp"),
            P("tp"),
            P("tp", None),
        ),
        out_specs=P("ctx", "tp"),
        check_vma=False,
    )
```

profile of v0, /device:TPU:0, one launch (start us, length us, event | category | flops | bytes accessed | tf_op | source)
XLA Modules:
  0.0 153.8 jit_solution(13737254396337837433)
XLA Ops:
  6.5 0.8 add_select_fusion
  7.4 2.1 %convolution_convert_fusion.2 = bf16[512,384]{1,0:T(8,128)(2,1)} fusion(bf16[256,384]{1,0:T(8,128)(2,1)} %param.14, s32[512]{0:T(512)S(1)} %add_select_fusion), kind=kOutput, calls=%fused_computation.16 | convolution fusion | flops 100990976 | bytes 591872 | tf_op jit(solution)/shard_map/dot_general | solution.py:45
  11.0 1.2 reduce-window.6
  12.8 12.5 %all-gather.1 = bf16[4,1,4]{2,1,0:T(2,128)(2,1)S(1)} all-gather(bf16[1,1,4]{2,1,0:T(2,128)(2,1)S(1)} %bitcast.73), channel_id=1, replica_groups=mesh['ctx'=4,'tp'=8] {'ctx'}, dimensions={0}, use_global_device_ids=true | all-gather | bytes 40 | tf_op jit(solution)/shard_map/all_gather | solution.py:14
  25.4 0.7 convert_element_type.86
  26.3 0.8 iota_compare_fusion
  27.8 17.5 %all-gather.4.cloned.1.call-done = bf16[512,3072]{1,0:T(8,128)(2,1)} async-done(((bf16[512,384]{1,0:T(8,128)(2,1)}), bf16[512,3072]{1,0:T(8,128)(2,1)}) %all-gather.4.cloned.1.call-update) | async-done | bytes 3145744 | tf_op jit(solution)/shard_map/all_gather | solution.py:46
  45.3 2.7 %fusion.1 = f32[512]{0:T(512)S(1)} fusion(bf16[512,3072]{1,0:T(8,128)(2,1)} %all-gather.4.cloned.1.call-done), kind=kLoop, calls=%fused_computation.5 | loop fusion | flops 4718080 | bytes 3147776 | tf_op jit(solution)/shard_map/reduce_sum | solution.py:48
  48.1 4.2 %multiply_convert_fusion.3 = bf16[512,512]{0,1:T(8,128)(2,1)S(1)} fusion(bf16[3072,512]{1,0:T(8,128)(2,1)} %param.17, bf16[512,3072]{1,0:T(8,128)(2,1)S(1)} %copy-done.2, f32[3072]{0:T(1024)S(1)} %convert_element_type.86, f32[512]{0:T(512)S(1)} %add_rsqrt_fusion.1), kind=kOutput, calls=%fused_computation.22 | convolution fusion | flops 1618214912 | bytes 6830080 | tf_op jit(solution)/shard_map/dot_general | solution.py:56
  52.3 2.0 %convolution_convert_fusion.1 = bf16[512,512]{0,1:T(8,128)(2,1)S(1)} fusion(bf16[3072,512]{1,0:T(8,128)(2,1)S(1)} %copy-done.3, bf16[512,3072]{1,0:T(8,128)(2,1)S(1)} %copy-done.2, f32[3072]{0:T(1024)S(1)} %convert_element_type.86, f32[512]{0:T(512)S(1)} %add_rsqrt_fusion.1), kind=kOutput, calls=%fused_computation.15 | convolution fusion | flops 1617166336 | bytes 6830080 | tf_op jit(solution)/shard_map/dot_general | solution.py:61
  54.7 16.6 %all-gather = bf16[16,128,128]{2,1,0:T(8,128)(2,1)} all-gather(bf16[4,128,128]{2,1,0:T(8,128)(2,1)S(1)} %convolution_convert_fusion.3), channel_id=2, replica_groups=mesh['ctx'=4,'tp'=8] {'ctx'}, dimensions={0}, use_global_device_ids=true | all-gather | bytes 655360 | tf_op jit(solution)/shard_map/all_gather | solution.py:14
  71.3 4.2 %while.14 = (s32[]{:T(128)}, f32[4,128,128]{2,1,0:T(8,128)S(1)}, s32[]{:T(128)}, bf16[4,4,128,128]{3,2,1,0:T(8,128)(2,1)}, bf16[4,4]{1,0:T(4,128)(2,1)S(1)}, /*index=5*/s32[]{:T(128)}, s32[]{:T(128)}) while((s32[]{:T(128)}, f32[4,128,128]{2,1,0:T(8,128)S(1)}, s32[]{:T(128)}, bf16[4,4,128,128]{3,2,1,0:T(8,128)(2,1)}, ...), condition=%wide.region_4.5_spmd.clone, body=%wide.region_3.4_spmd.clone.sunk | while | flops 327688 | bytes 655513 | solution.py:27
  71.3 1.0 fusion.36
  72.3 1.0 fusion.36
  73.4 1.0 fusion.36
  74.5 1.0 fusion.36
  75.5 5.7 %multiply_convert_fusion.4 = bf16[512,512]{0,1:T(8,128)(2,1)} fusion(bf16[3072,512]{1,0:T(8,128)(2,1)} %param.16, bf16[512,3072]{1,0:T(8,128)(2,1)} %all-gather.4.cloned.1.call-done, f32[3072]{0:T(1024)S(1)} %convert_element_type.86, f32[512]{0:T(512)S(1)} %add_rsqrt_fusion.1), kind=kOutput, calls=%fused_computation.23 | convolution fusion | flops 1618214912 | bytes 6830080 | tf_op jit(solution)/shard_map/dot_general | solution.py:51
  81.2 4.5 %fusion.5 = f32[512,4,128]{0,2,1:T(8,128)} fusion(bf16[512,4,128]{0,2,1:T(8,128)(2,1)} %bitcast.77, bf16[512,4,128]{0,2,1:T(8,128)(2,1)} %bitcast.65, bf16[512,4,128]{0,2,1:T(8,128)(2,1)} %bitcast.75, f32[4,512]{1,0:T(4,128)S(1)} %bitcast.70, pred[512,512]{1,0:T(8,128)(4,1)} %iota_compare_fusion), kind=kOutput, calls=%fused_computation.11 | convolution fusion | flops 542113792 | bytes 2891776 | tf_op jit(solution)/shard_map/hts,shd->thd/dot_general | solution.py:74
  85.7 2.1 %multiply_reduce_fusion = (f32[512,4]{0,1:T(4,128)S(1)}, f32[512,4,128]{0,2,1:T(8,128)S(1)}) fusion(f32[512,4,128]{0,2,1:T(8,128)} %fusion.5, f32[4,128,128]{2,1,0:T(8,128)S(1)} %get-tuple-element.99, bf16[512,4,128]{0,2,1:T(8,128)(2,1)} %bitcast.66, f32[512,4]{0,1:T(4,128)S(1)} %get-tuple-element.128), kind=kOutput, calls=%fused_computation.19 | convolution fusion | flops 403699712 | bytes 2899968 | tf_op jit(solution)/shard_map/thd,hde->the/dot_general | solution.py:89
  88.0 3.5 %convolution_convert_fusion = bf16[512,3072]{1,0:T(8,128)(2,1)} fusion(bf16[512,512]{0,1:T(8,128)(2,1)S(1)} %bitcast.64, bf16[512,3072]{1,0:T(8,128)(2,1)S(1)} %copy-done), kind=kOutput, calls=%fused_computation.8 | convolution fusion | flops 1612185600 | bytes 6815744 | tf_op jit(solution)/shard_map/dot_general | solution.py:97
  91.5 4.7 %copy.46 = bf16[512,3072]{0,1:T(8,128)(2,1)} copy(bf16[512,3072]{1,0:T(8,128)(2,1)} %convolution_convert_fusion) | data formatting | bytes 6291456
  96.2 47.1 %reduce-scatter.4.cloned.1.call-done = bf16[384,512]{1,0:T(8,128)(2,1)} async-done(((bf16[3072,512]{1,0:T(8,128)(2,1)}), bf16[384,512]{1,0:T(8,128)(2,1)}) %reduce-scatter.4.cloned.1.call-update) | async-done | bytes 393232
  143.3 1.9 %copy.47 = bf16[512,384]{1,0:T(8,128)(2,1)} copy(bf16[512,384]{0,1:T(8,128)(2,1)} %bitcast.67) | data formatting | bytes 786432
  145.2 1.8 %add_convert_fusion = bf16[512,384]{1,0:T(8,128)(2,1)} fusion(bf16[512,384]{1,0:T(8,128)(2,1)} %copy.47, bf16[512,384]{1,0:T(8,128)(2,1)S(1)} %copy-done.1), kind=kLoop, calls=%fused_computation.24 | loop fusion | flops 786432 | bytes 1179648 | tf_op jit(solution)/shard_map/convert_element_type | solution.py:105
  (37 shorter events, 3.7 us)
Async XLA Ops:
  6.5 81.4 %copy-start = (bf16[512,3072]{1,0:T(8,128)(2,1)S(1)}, bf16[512,3072]{1,0:T(8,128)(2,1)}, u32[]{:S(2)}) copy-start(bf16[512,3072]{1,0:T(8,128)(2,1)} %param.21) | copy-start | bytes 9437188
  6.5 38.7 %all-gather.4.cloned.1.call-start = ((), (), s32[]{:S(2)}) async-start(), calls=%async_computation.1 | async-start | bytes 3538944 | tf_op jit(solution)/shard_map/all_gather | solution.py:46
  9.5 133.7 %reduce-scatter.4.cloned.1.call-start = ((), (), s32[]{:S(2)}) async-start(), calls=%async_computation.2 | async-start | bytes 3538944
  45.3 2.8 %copy-start.2 = (bf16[512,3072]{1,0:T(8,128)(2,1)S(1)}, bf16[512,3072]{1,0:T(8,128)(2,1)}, u32[]{:S(2)}) copy-start(bf16[512,3072]{1,0:T(8,128)(2,1)} %all-gather.4.cloned.1.call-done) | copy-start | bytes 9437188
  48.1 4.2 %copy-start.3 = (bf16[3072,512]{1,0:T(8,128)(2,1)S(1)}, bf16[3072,512]{1,0:T(8,128)(2,1)}, u32[]{:S(2)}) copy-start(bf16[3072,512]{1,0:T(8,128)(2,1)} %param.18) | copy-start | bytes 9437188
  52.3 2.1 %copy-start.4 = (bf16[512,512]{0,1:T(8,128)(2,1)}, bf16[512,512]{0,1:T(8,128)(2,1)S(1)}, u32[]{:S(2)}) copy-start(bf16[512,512]{0,1:T(8,128)(2,1)S(1)} %multiply_convert_fusion.3) | copy-start | bytes 1572868
  54.4 16.9 %copy-start.5 = (bf16[512,512]{0,1:T(8,128)(2,1)}, bf16[512,512]{0,1:T(8,128)(2,1)S(1)}, u32[]{:S(2)}) copy-start(bf16[512,512]{0,1:T(8,128)(2,1)S(1)} %convolution_convert_fusion.1) | copy-start | bytes 1572868
  96.2 49.0 %copy-start.1 = (bf16[512,384]{1,0:T(8,128)(2,1)S(1)}, bf16[512,384]{1,0:T(8,128)(2,1)}, u32[]{:S(2)}) copy-start(bf16[512,384]{1,0:T(8,128)(2,1)} %convolution_convert_fusion.2) | copy-start | bytes 1179652
Sparse Core Ops, SparseCore 0:
  9.7 35.5 all-gather.3
  96.3 46.8 reduce-scatter.3
where the time goes:
time: 154 us
  waiting for transfers between devices  64.6 us (42%)
  blocking collectives  29.1 us (19%)
  matrix products  24.5 us (16%)
  other arithmetic  14.8 us (10%)
  between operations  13.5 us (9%)
  local copies, waits for them, and re-layouts  7.21 us (5%)
    unnamed x3, waiting for transfers between devices  47.1 us
    all_gather x2, blocking collectives, entering(): lax.all_gather(part.astype(kind), axis)  29.1 us
    all_gather x1, waiting for transfers between devices, per_device(): full_x = lax.all_gather(local_x, 'tp', axis=1, tiled=True)  17.5 us
    unnamed x16, local copies, waits for them, and re-layouts  6.69 us
    dot_general x1, matrix products, per_device(): jnp.dot(normed, w_query, preferred_element_type=jnp.float32)  5.71 us
    dot_general x1, matrix products, per_device(): jnp.einsum('hts,shd->thd', weights, value_rows, preferred_element_type=jn...  4.47 us
    dot_general x1, matrix products, per_device(): jnp.dot(normed, w_key, preferred_element_type=jnp.float32)  4.19 us
    select_n x4, other arithmetic, hop(): return jax.tree.map(lambda a, b: jnp.where(reached, a, b), new, before)  4.06 us
  transfers between devices with their start and end apart: 2, of which 2 were waited for; matrix products, arithmetic and copies ran while one was open for 4% of the time, Pallas kernels for 0%

commit v1 on v0

v1 whole, which is shorter than its diff:
```python
import functools
import math

import jax
import jax.numpy as jnp
from jax import lax
from jax.experimental import pallas as pl
from jax.experimental.pallas import tpu as pltpu
from jax.sharding import PartitionSpec as P

MESH = pl.DeviceIdType.MESH
LOG_KEEP = math.log(0.75)
F32, BF16 = jnp.float32, jnp.bfloat16
ORDER = (1, 3, 5, 7, 0, 2, 4, 6)


def dot(a, b):
    return jnp.dot(a, b, preferred_element_type=F32)


def dot_rows(a, b):
    return lax.dot_general(a, b, (((0,), (0,)), ((), ())), preferred_element_type=F32)


def dot_lanes(a, b):
    return lax.dot_general(a, b, (((1,), (1,)), ((), ())), preferred_element_type=F32)


def layer(
    n_ctx, chunk,
    ids_ref, marks_ref, table_ref, gain_ref, wq_ref, wk_ref, wv_ref, idx_ref, ogain_ref, wout_ref,
    out_ref,
    full, normed, w_in, w_o, qkv, hot, state, msg, msgs, att, keep0, s0, r0, keep1, s1, r1, keep2, s2, r2,
    load_sem, ag_send, ag_recv, ctx_send, ctx_recv, rs_send, rs_recv,
):
    me, place = lax.axis_index("tp"), lax.axis_index("ctx")
    buckets, width = table_ref.shape
    rows = ids_ref.shape[1]
    tiles, model, tile = w_in.shape
    heads, hw = state.shape[0], state.shape[1]
    per = tile // hw
    group = heads // per
    bits = [(me // (1 << k)) % 2 for k in range(3)]

    def other(p):
        index = me
        for k in range(3):
            if (p >> k) & 1:
                index = index + (1 - 2 * bits[k]) * (1 << k)
        return index

    sib, xp, yp, diag = other(1), other(2), other(4), other(6)

    loads = []
    for n in range(tiles):
        source = (wq_ref, wk_ref, wv_ref)[n // group]
        loads.append(pltpu.make_async_copy(
            source.at[:, pl.ds((n % group) * tile, tile)], w_in.at[n], load_sem.at[n]))
    for at, p in enumerate(ORDER):
        first = pl.multiple_of(other(p) * width, 128)
        loads.append(pltpu.make_async_copy(
            wout_ref.at[:, pl.ds(first, width)],
            w_o.at[at // 2, :, pl.ds((at % 2) * width, width)], load_sem.at[tiles + at]))
    for load in loads:
        load.start()

    barrier = pltpu.get_barrier_semaphore()
    for peer in (sib, xp, yp):
        pl.semaphore_signal(barrier, inc=1, device_id={"tp": peer}, device_id_type=MESH)
    for d in range(1, n_ctx):
        pl.semaphore_signal(
            barrier, inc=1, device_id={"ctx": lax.rem(place + d, n_ctx)}, device_id_type=MESH)
    pl.semaphore_wait(barrier, 3 + n_ctx - 1)

    half = buckets // 2
    lo, hi = pl.ds(0, half), pl.ds(half, half)

    def ag(k, src, dst, peer):
        return pltpu.make_async_remote_copy(
            src_ref=src, dst_ref=dst, send_sem=ag_send.at[k], recv_sem=ag_recv.at[k],
            device_id={"tp": peer}, device_id_type=MESH)

    gathers = [
        ag(0, table_ref.at[lo], full.at[me, lo], xp),
        ag(1, table_ref.at[hi], full.at[me, hi], yp),
        ag(2, table_ref, full.at[me], sib),
        ag(3, table_ref.at[hi], full.at[me, hi], xp),
        ag(4, table_ref.at[lo], full.at[me, lo], yp),
        ag(5, full.at[xp, lo], full.at[xp, lo], yp),
        ag(6, full.at[yp, hi], full.at[yp, hi], xp),
        ag(7, full.at[xp, lo], full.at[xp, lo], sib),
        ag(8, full.at[yp, hi], full.at[yp, hi], sib),
        ag(9, full.at[xp, hi], full.at[xp, hi], sib),
        ag(10, full.at[yp, lo], full.at[yp, lo], sib),
        ag(11, full.at[diag, lo], full.at[diag, lo], sib),
        ag(12, full.at[diag, hi], full.at[diag, hi], sib),
    ]
    for k in range(5):
        gathers[k].start()
    full[me] = table_ref[...]

    hashed = ((ids_ref[...] * 7919 + 13) & (buckets - 1)).astype(F32)
    upto = lax.broadcasted_iota(jnp.int32, (rows, rows), 0) <= lax.broadcasted_iota(
        jnp.int32, (rows, rows), 1)
    mark8 = jnp.broadcast_to(marks_ref[...].astype(F32), (8, rows)).astype(BF16)
    count = dot(mark8, jnp.where(upto, 1.0, 0.0).astype(BF16))
    sub = lax.broadcasted_iota(jnp.int32, (8, rows), 0)
    turned = jnp.where(sub == 0, jnp.broadcast_to(hashed, (8, rows)), count).T
    hash_col, count_col = turned[:, 0:1], turned[:, 1:2]
    hot[...] = jnp.where(
        lax.broadcasted_iota(jnp.int32, (rows, buckets), 1).astype(F32) == hash_col, 1.0, 0.0
    ).astype(BF16)
    index8 = jnp.zeros((8, rows), F32)
    for h in range(heads):
        index8 = jnp.where(sub == h, idx_ref[h].astype(F32), index8)
    rates = jnp.exp2(-0.25 * index8)
    steps = (lax.broadcasted_iota(jnp.int32, (8, rows), 1) + 1).astype(F32)
    cum = count * LOG_KEEP - steps * rates
    total = cum[:, rows - 1:rows]
    msg[:, :buckets] = dot(jnp.exp(total - cum).astype(BF16), hot[...])
    msg[:, buckets:] = jnp.broadcast_to(total, (8, 128))

    sends = []
    for d in range(1, n_ctx):
        sends.append(pltpu.make_async_remote_copy(
            src_ref=msg, dst_ref=msgs.at[d - 1], send_sem=ctx_send.at[d - 1],
            recv_sem=ctx_recv.at[d - 1],
            device_id={"ctx": lax.rem(place + d, n_ctx)}, device_id_type=MESH))
        sends[-1].start()

    gathers[0].wait_recv()
    gathers[5].start()
    gathers[7].start()
    gathers[1].wait_recv()
    gathers[6].start()
    gathers[8].start()
    gathers[3].wait_recv()
    gathers[9].start()
    gathers[4].wait_recv()
    gathers[10].start()

    incoming, passed = jnp.zeros((8, buckets), F32), jnp.zeros((8, 1), F32)
    for d in range(1, n_ctx):
        sends[d - 1].wait_recv()
        reached = jnp.where(d <= place, 1.0, 0.0)
        incoming = incoming + reached * jnp.exp(passed) * msgs[d - 1, :, :buckets]
        passed = passed + msgs[d - 1, :, buckets:buckets + 1]
    incoming_col = incoming.T

    gathers[5].wait_recv()
    gathers[11].start()
    gathers[6].wait_recv()
    gathers[12].start()
    for k in (2, 7, 8, 9, 10, 11, 12):
        gathers[k].wait_recv()

    n_tp = full.shape[0]
    squares = jnp.zeros((buckets, 1), F32)
    for j in range(n_tp):
        x = full[j].astype(F32)
        squares = squares + jnp.sum(x * x, axis=1, keepdims=True)
    inv = lax.rsqrt(squares / model + 1e-05)
    for j in range(n_tp):
        cols = slice(j * width, (j + 1) * width)
        normed[:, cols] = (full[j].astype(F32) * inv * gain_ref[:, cols].astype(F32)).astype(BF16)
    for n in range(tiles):
        loads[n].wait()

    @pl.loop(0, 2 * group)
    def _(n):
        y = dot(normed[...], w_in[n])
        qkv[n] = (y / (1.0 + jnp.exp(-y))).astype(BF16)

    @pl.loop(2 * group, tiles)
    def _(n):
        qkv[n] = dot(normed[...], w_in[n]).astype(BF16)

    for h in range(heads):
        lanes = slice((h % per) * hw, (h % per + 1) * hw)
        key, value = qkv[group + h // per, :, lanes], qkv[2 * group + h // per, :, lanes]
        state[h] = dot_rows((key.astype(F32) * incoming_col[:, h:h + 1]).astype(BF16), value)
    for load in loads[tiles:]:
        load.wait()

    n_chunks = rows // chunk
    part = chunk // 2
    t_at = lax.broadcasted_iota(jnp.int32, (chunk, chunk), 0)
    s_at = lax.broadcasted_iota(jnp.int32, (chunk, chunk), 1)
    ahead = (t_at - s_at).astype(F32)
    step_col = (lax.broadcasted_iota(jnp.int32, (chunk, 1), 0) + 1).astype(F32)

    def rs(k, src, dst, peer):
        return pltpu.make_async_remote_copy(
            src_ref=src, dst_ref=dst, send_sem=rs_send.at[k], recv_sem=rs_recv.at[k],
            device_id={"tp": peer}, device_id_type=MESH)

    stage0 = [rs(5 * c, s0.at[c], r0.at[c], sib) for c in range(n_chunks)]
    stage1 = [[rs(5 * c + 1 + f, s1.at[c, f], r1.at[c, f], (xp, yp)[f]) for f in range(2)]
              for c in range(n_chunks)]
    stage2 = [[rs(5 * c + 3 + f, s2.at[c, f], r2.at[c, f], (yp, xp)[f]) for f in range(2)]
              for c in range(n_chunks)]

    def attend(c):
        at = slice(c * chunk, (c + 1) * chunk)
        one = hot[at]
        picked = [dot(one, qkv[n]).astype(BF16) for n in range(tiles)]
        here_col, here_row = count_col[at], count[0:1, at]
        before = count_col[c * chunk - 1:c * chunk] if c else jnp.zeros((1, 1), F32)
        last = count_col[(c + 1) * chunk - 1:(c + 1) * chunk]
        gap = jnp.where(t_at >= s_at, (here_col - here_row) * LOG_KEEP, -1e30)
        for h in range(heads):
            lanes = slice((h % per) * hw, (h % per + 1) * hw)
            query = picked[h // per][:, lanes]
            key = picked[group + h // per][:, lanes]
            value = picked[2 * group + h // per][:, lanes]
            rate = rates[h:h + 1, 0:1]
            weights = (dot_lanes(query, key) * jnp.exp(gap - ahead * rate)).astype(BF16)
            carried = state[h]
            begun = jnp.exp((here_col - before) * LOG_KEEP - step_col * rate)
            attended = dot(weights, value) + begun * dot(query, carried.astype(BF16))
            if c < n_chunks - 1:
                left = jnp.exp((last - here_col) * LOG_KEEP - (chunk - step_col) * rate)
                decayed = (key.astype(F32) * left).astype(BF16)
                whole = jnp.exp((last - before) * LOG_KEEP - chunk * rate)
                state[h] = whole * carried + dot_rows(decayed, value)
            scale = lax.rsqrt(jnp.mean(attended * attended, axis=1, keepdims=True) + 1e-06)
            wide = slice(h * hw, (h + 1) * hw)
            att[:, wide] = (attended * scale * ogain_ref[:, wide].astype(F32)).astype(BF16)
        for pair in range(2):
            s0[c, pair] = dot(att[...], w_o[pair]).astype(BF16)
        stage0[c].start()
        for pair in range(2):
            keep0[c, pair] = dot(att[...], w_o[2 + pair])

    def after0(c):
        stage0[c].wait_recv()
        for f in range(2):
            cut = slice(f * part, (f + 1) * part)
            sums = [keep0[c, q // 2, cut, (q % 2) * width:(q % 2 + 1) * width]
                    + r0[c, q // 2, cut, (q % 2) * width:(q % 2 + 1) * width].astype(F32)
                    for q in range(4)]
            go, stay = (((1, 3), (0, 2)), ((2, 3), (0, 1)))[f]
            for i in range(2):
                s1[c, f, i] = sums[go[i]].astype(BF16)
                keep1[c, f, i] = sums[stay[i]]
            stage1[c][f].start()

    def after1(c):
        for f in range(2):
            stage1[c][f].wait_recv()
            s2[c, f] = (keep1[c, f, 1] + r1[c, f, 1].astype(F32)).astype(BF16)
            stage2[c][f].start()
            keep2[c, f] = keep1[c, f, 0] + r1[c, f, 0].astype(F32)

    def after2(c):
        for f in range(2):
            stage2[c][f].wait_recv()
            at = slice(c * chunk + f * part, c * chunk + (f + 1) * part)
            residual = dot(hot[at], table_ref[...])
            out_ref[at, :] = (residual + (keep2[c, f] + r2[c, f].astype(F32))).astype(BF16)

    for step in range(n_chunks + 3):
        if step < n_chunks:
            attend(step)
        if 0 <= step - 1 < n_chunks:
            after0(step - 1)
        if 0 <= step - 2 < n_chunks:
            after1(step - 2)
        if 0 <= step - 3 < n_chunks:
            after2(step - 3)

    for copy in gathers + sends:
        copy.wait_send()
    for c in range(n_chunks):
        stage0[c].wait_send()
        for f in range(2):
            stage1[c][f].wait_send()
            stage2[c][f].wait_send()


def per_device(n_ctx, n_tp, token_ids, marks, table, norm_gain, w_query, w_key, w_value, decay_idx, out_gain, w_out):
    if n_tp != len(ORDER):
        raise ValueError("tp size")
    rows, (buckets, width) = token_ids.shape[0], table.shape
    model, columns = w_query.shape
    heads = decay_idx.shape[0]
    hw = columns // heads
    tile = 2 * hw
    tiles = 3 * columns // tile
    chunk = rows // 4
    n_chunks = rows // chunk
    part = chunk // 2
    vmem, hbm = pl.BlockSpec(memory_space=pltpu.VMEM), pl.BlockSpec(memory_space=pl.ANY)
    return pl.pallas_call(
        functools.partial(layer, n_ctx, chunk),
        out_shape=jax.ShapeDtypeStruct((rows, width), BF16),
        in_specs=[vmem, vmem, vmem, vmem, hbm, hbm, hbm,
                  pl.BlockSpec(memory_space=pltpu.SMEM), vmem, hbm],
        out_specs=vmem,
        scratch_shapes=[
            pltpu.VMEM((n_tp, buckets, width), BF16),
            pltpu.VMEM((buckets, model), BF16),
            pltpu.VMEM((tiles, model, tile), BF16),
            pltpu.VMEM((n_tp // 2, columns, 2 * width), BF16),
            pltpu.VMEM((tiles, buckets, tile), BF16),
            pltpu.VMEM((rows, buckets), BF16),
            pltpu.VMEM((heads, hw, hw), F32),
            pltpu.VMEM((8, buckets + 128), F32),
            pltpu.VMEM((max(n_ctx - 1, 1), 8, buckets + 128), F32),
            pltpu.VMEM((chunk, columns), BF16),
            pltpu.VMEM((n_chunks, 2, chunk, 2 * width), F32),
            pltpu.VMEM((n_chunks, 2, chunk, 2 * width), BF16),
            pltpu.VMEM((n_chunks, 2, chunk, 2 * width), BF16),
            pltpu.VMEM((n_chunks, 2, 2, part, width), F32),
            pltpu.VMEM((n_chunks, 2, 2, part, width), BF16),
            pltpu.VMEM((n_chunks, 2, 2, part, width), BF16),
            pltpu.VMEM((n_chunks, 2, part, width), F32),
            pltpu.VMEM((n_chunks, 2, part, width), BF16),
            pltpu.VMEM((n_chunks, 2, part, width), BF16),
            pltpu.SemaphoreType.DMA((tiles + n_tp,)),
            pltpu.SemaphoreType.DMA((13,)),
            pltpu.SemaphoreType.DMA((13,)),
            pltpu.SemaphoreType.DMA((max(n_ctx - 1, 1),)),
            pltpu.SemaphoreType.DMA((max(n_ctx - 1, 1),)),
            pltpu.SemaphoreType.DMA((5 * n_chunks,)),
            pltpu.SemaphoreType.DMA((5 * n_chunks,)),
        ],
        compiler_params=pltpu.CompilerParams(
            collective_id=0, has_side_effects=True, vmem_limit_bytes=56 * 2**20),
        name="layer",
    )(
        token_ids.reshape(1, rows), marks.reshape(1, rows), table, norm_gain.reshape(1, model),
        w_query, w_key, w_value, decay_idx, out_gain.reshape(1, columns), w_out,
    )


def solution(mesh):
    return jax.shard_map(
        functools.partial(per_device, mesh.shape["ctx"], mesh.shape["tp"]),
        mesh=mesh,
        in_specs=(
            P("ctx"), P("ctx"), P(None, "tp"), P(), P(None, "tp"), P(None, "tp"), P(None, "tp"),
            P("tp"), P("tp"), P("tp", None),
        ),
        out_specs=P("ctx", "tp"),
        check_vma=False,
    )
```

time: 154 us -> 47.1 us (0.31)
  waiting for transfers between devices: 64.6 us -> 0 us
  Pallas kernels: 0 us -> 42.5 us
  blocking collectives: 29.1 us -> 0 us
  matrix products: 24.5 us -> 0 us
  other arithmetic: 14.8 us -> 0 us
  between operations: 13.5 us -> 0.01 us
  local copies, waits for them, and re-layouts: 7.21 us -> 4.34 us
    unnamed x3 -> x0, waiting for transfers between devices: 47.1 us -> none
    pallas_call x0 -> x1, Pallas kernels: none -> 42.5 us  [per_device(): pl.pallas_call(functools.partial(layer, n_ctx, chunk), out_shape=jax.Shap...]
    all_gather x2 -> x0, blocking collectives: 29.1 us -> none  [entering(): lax.all_gather(part.astype(kind), axis)]
    dot_general x8 -> x0, matrix products: 24.5 us -> none  [the longest x1 5.71 us: per_device(): jnp.dot(normed, w_query, preferred_element_type=jnp.float32)]
    all_gather x1 -> x0, waiting for transfers between devices: 17.5 us -> none  [per_device(): full_x = lax.all_gather(local_x, 'tp', axis=1, tiled=True)]
    unnamed x16 -> x1, local copies, waits for them, and re-layouts: 6.69 us -> 1.78 us
    select_n x5 -> x0, other arithmetic: 4.9 us -> none  [the longest x4 4.06 us: hop(): return jax.tree.map(lambda a, b: jnp.where(reached, a, b), new, before)]
    reduce_sum x1 -> x0, other arithmetic: 2.73 us -> none  [per_device(): jnp.mean(x_float * x_float, axis=1, keepdims=True) + 1e-05]
  transfers between devices with their start and end apart: 2 -> 0, of which waited for: 2 -> 0; matrix products, arithmetic and copies ran while one was open for 4% -> 0% of each run, Pallas kernels for 0% -> 0%
where the time goes in v1:
time: 47.1 us; the launch traced here: 46.8 us
  Pallas kernels  42.5 us (90%)
  local copies, waits for them, and re-layouts  4.34 us (9%)
    pallas_call x1, Pallas kernels, per_device(): pl.pallas_call(functools.partial(layer, n_ctx, chunk), out_shape=jax.Shap...  42.5 us
    unnamed x1, local copies, waits for them, and re-layouts  1.78 us
    reshape x1, local copies, waits for them, and re-layouts, per_device(): norm_gain.reshape(1, model)  1.3 us
    reshape x1, local copies, waits for them, and re-layouts, per_device(): out_gain.reshape(1, columns)  1.26 us

profile of v1, /device:TPU:0, one launch (start us, length us, event | category | flops | bytes accessed | tf_op | source)
XLA Modules:
  0.0 46.8 jit_solution(1442425341998820848)
XLA Ops:
  0.0 1.3 %reshape.15.ogain_ref = bf16[1,512]{1,0:T(2,128)(2,1)} reshape(bf16[512]{0:T(512)(128)(2,1)} %param.18) | data formatting | bytes 2048 | tf_op jit(solution)/shard_map/reshape | solution.py:333
  1.3 1.3 %reshape.14.gain_ref = bf16[1,3072]{1,0:T(2,128)(2,1)} reshape(bf16[3072]{0:T(1024)(128)(2,1)} %param.13) | data formatting | bytes 12288 | tf_op jit(solution)/shard_map/reshape | solution.py:332
  2.6 42.5 %layer.1 = bf16[512,384]{1,0:T(8,128)(2,1)} custom-call(s32[1,512]{1,0:T(1,128)} %bitcast.2, s32[1,512]{1,0:T(1,128)} %bitcast.3, bf16[256,384]{1,0:T(8,128)(2,1)} %table_ref.1, bf16[1,3072]{1,0:T(2,128)(2,1)} %reshape.14.gain_ref, bf16[3072,512]{1,0:T(8,128)(2,1)} %wq_ref.1, bf16[3072,512]{1,0:T(8,128)(2,1)} %wk_ref.1, bf16[3072,512]{1,0:T(8,128)(2,1)} %wv_ref.1, ...), custom_call_target="tpu_custom_call" | custom-call | tf_op jit(solution)/shard_map/layer/pallas_call | solution.py:294
  45.0 1.8 %copy.12 = bf16[512,384]{1,0:T(8,128)(2,1)} copy(bf16[512,384]{1,0:T(8,128)(2,1)} %layer.1) | data formatting | bytes 786432

commit v2 on v1

--- a/solution.py
+++ b/solution.py
@@ -30,8 +30,8 @@
     n_ctx, chunk,
     ids_ref, marks_ref, table_ref, gain_ref, wq_ref, wk_ref, wv_ref, idx_ref, ogain_ref, wout_ref,
     out_ref,
-    full, normed, w_in, w_o, qkv, hot, state, msg, msgs, att, keep0, s0, r0, keep1, s1, r1, keep2, s2, r2,
-    load_sem, ag_send, ag_recv, ctx_send, ctx_recv, rs_send, rs_recv,
+    sq_out, sq_in, full, gains, normed, acc, w_in, w_o, qkv, hot, state, msg, msgs, att, keep0, s0, r0, keep1, s1, r1, keep2, s2, r2,
+    sq_send, sq_recv, load_sem, ag_send, ag_recv, ctx_send, ctx_recv, rs_send, rs_recv,
 ):
     me, place = lax.axis_index("tp"), lax.axis_index("ctx")
     buckets, width = table_ref.shape
@@ -51,6 +51,14 @@
 
     sib, xp, yp, diag = other(1), other(2), other(4), other(6)
 
+    barrier = pltpu.get_barrier_semaphore()
+    n_tp = full.shape[0]
+    for d in range(1, n_tp):
+        pl.semaphore_signal(
+            barrier, inc=1, device_id={"tp": lax.rem(me + d, n_tp)}, device_id_type=MESH)
+    for d in range(1, n_ctx):
+        pl.semaphore_signal(
+            barrier, inc=1, device_id={"ctx": lax.rem(place + d, n_ctx)}, device_id_type=MESH)
     loads = []
     for n in range(tiles):
         source = (wq_ref, wk_ref, wv_ref)[n // group]
@@ -64,13 +72,10 @@
     for load in loads:
         load.start()
 
-    barrier = pltpu.get_barrier_semaphore()
-    for peer in (sib, xp, yp):
-        pl.semaphore_signal(barrier, inc=1, device_id={"tp": peer}, device_id_type=MESH)
-    for d in range(1, n_ctx):
-        pl.semaphore_signal(
-            barrier, inc=1, device_id={"ctx": lax.rem(place + d, n_ctx)}, device_id_type=MESH)
-    pl.semaphore_wait(barrier, 3 + n_ctx - 1)
+    own = table_ref[...].astype(F32)
+    sq_out[...] = jnp.broadcast_to(
+        jnp.sum(own * own, axis=1, keepdims=True), (buckets, 128)).T[:8]
+    pl.semaphore_wait(barrier, n_tp - 1 + n_ctx - 1)
 
     half = buckets // 2
     lo, hi = pl.ds(0, half), pl.ds(half, half)
@@ -95,9 +100,21 @@
         ag(11, full.at[diag, lo], full.at[diag, lo], sib),
         ag(12, full.at[diag, hi], full.at[diag, hi], sib),
     ]
-    for k in range(5):
+    for k in range(3):
         gathers[k].start()
+    shares = []
+    for d in range(1, n_tp):
+        shares.append(pltpu.make_async_remote_copy(
+            src_ref=sq_out, dst_ref=sq_in.at[d - 1], send_sem=sq_send.at[d - 1],
+            recv_sem=sq_recv.at[d - 1],
+            device_id={"tp": lax.rem(me + d, n_tp)}, device_id_type=MESH))
+        shares[-1].start()
     full[me] = table_ref[...]
+    for j in range(n_tp):
+        gains[j] = gain_ref[j * width:(j + 1) * width].astype(F32).reshape(1, width)
+
+    for k in (3, 4):
+        gathers[k].start()
 
     hashed = ((ids_ref[...] * 7919 + 13) & (buckets - 1)).astype(F32)
     upto = lax.broadcasted_iota(jnp.int32, (rows, rows), 0) <= lax.broadcasted_iota(
@@ -128,12 +145,34 @@
             device_id={"ctx": lax.rem(place + d, n_ctx)}, device_id_type=MESH))
         sends[-1].start()
 
+    def scale(block, k):
+        first = block - bits[0]
+        for i in range(2):
+            x = full[first + i].astype(F32)
+            normed[k, :, i * width:(i + 1) * width] = (x * inv * gains[first + i]).astype(BF16)
+        return pl.ds(pl.multiple_of(first * width, 128), 2 * width)
+
     gathers[0].wait_recv()
     gathers[5].start()
     gathers[7].start()
     gathers[1].wait_recv()
     gathers[6].start()
     gathers[8].start()
+    squares = sq_out[...]
+    for d in range(1, n_tp):
+        shares[d - 1].wait_recv()
+        squares = squares + sq_in[d - 1]
+    inv_row = lax.rsqrt(squares / model + 1e-05)
+    inv = jnp.broadcast_to(inv_row[0:1], (128, buckets)).T[:, 0:1]
+    gathers[2].wait_recv()
+    span = scale(me, 0)
+    for n in range(tiles):
+        loads[n].wait()
+
+    @pl.loop(0, tiles)
+    def _(n):
+        acc[n] = dot(normed[0], w_in[n, span])
+
     gathers[3].wait_recv()
     gathers[9].start()
     gathers[4].wait_recv()
@@ -147,33 +186,38 @@
         passed = passed + msgs[d - 1, :, buckets:buckets + 1]
     incoming_col = incoming.T
 
+    gathers[7].wait_recv()
+    gathers[9].wait_recv()
+    span1 = scale(xp, 1)
+
+    @pl.loop(0, tiles)
+    def _(n):
+        acc[n] += dot(normed[1], w_in[n, span1])
+
     gathers[5].wait_recv()
     gathers[11].start()
     gathers[6].wait_recv()
     gathers[12].start()
-    for k in (2, 7, 8, 9, 10, 11, 12):
-        gathers[k].wait_recv()
-
-    n_tp = full.shape[0]
-    squares = jnp.zeros((buckets, 1), F32)
-    for j in range(n_tp):
-        x = full[j].astype(F32)
-        squares = squares + jnp.sum(x * x, axis=1, keepdims=True)
-    inv = lax.rsqrt(squares / model + 1e-05)
-    for j in range(n_tp):
-        cols = slice(j * width, (j + 1) * width)
-        normed[:, cols] = (full[j].astype(F32) * inv * gain_ref[:, cols].astype(F32)).astype(BF16)
-    for n in range(tiles):
-        loads[n].wait()
+    gathers[8].wait_recv()
+    gathers[10].wait_recv()
+    span2 = scale(yp, 0)
+
+    @pl.loop(0, tiles)
+    def _(n):
+        acc[n] += dot(normed[0], w_in[n, span2])
+
+    gathers[11].wait_recv()
+    gathers[12].wait_recv()
+    span3 = scale(diag, 1)
 
     @pl.loop(0, 2 * group)
     def _(n):
-        y = dot(normed[...], w_in[n])
+        y = acc[n] + dot(normed[1], w_in[n, span3])
         qkv[n] = (y / (1.0 + jnp.exp(-y))).astype(BF16)
 
     @pl.loop(2 * group, tiles)
     def _(n):
-        qkv[n] = dot(normed[...], w_in[n]).astype(BF16)
+        qkv[n] = (acc[n] + dot(normed[1], w_in[n, span3])).astype(BF16)
 
     for h in range(heads):
         lanes = slice((h % per) * hw, (h % per + 1) * hw)
@@ -225,7 +269,7 @@
                 state[h] = whole * carried + dot_rows(decayed, value)
             scale = lax.rsqrt(jnp.mean(attended * attended, axis=1, keepdims=True) + 1e-06)
             wide = slice(h * hw, (h + 1) * hw)
-            att[:, wide] = (attended * scale * ogain_ref[:, wide].astype(F32)).astype(BF16)
+            att[:, wide] = (attended * scale * ogain_ref[wide].astype(F32).reshape(1, hw)).astype(BF16)
         for pair in range(2):
             s0[c, pair] = dot(att[...], w_o[pair]).astype(BF16)
         stage0[c].start()
@@ -269,7 +313,7 @@
         if 0 <= step - 3 < n_chunks:
             after2(step - 3)
 
-    for copy in gathers + sends:
+    for copy in gathers + sends + shares:
         copy.wait_send()
     for c in range(n_chunks):
         stage0[c].wait_send()
@@ -298,8 +342,12 @@
                   pl.BlockSpec(memory_space=pltpu.SMEM), vmem, hbm],
         out_specs=vmem,
         scratch_shapes=[
+            pltpu.VMEM((8, buckets), F32),
+            pltpu.VMEM((n_tp - 1, 8, buckets), F32),
             pltpu.VMEM((n_tp, buckets, width), BF16),
-            pltpu.VMEM((buckets, model), BF16),
+            pltpu.VMEM((n_tp, 1, width), F32),
+            pltpu.VMEM((2, buckets, 2 * width), BF16),
+            pltpu.VMEM((tiles, buckets, tile), F32),
             pltpu.VMEM((tiles, model, tile), BF16),
             pltpu.VMEM((n_tp // 2, columns, 2 * width), BF16),
             pltpu.VMEM((tiles, buckets, tile), BF16),
@@ -317,6 +365,8 @@
             pltpu.VMEM((n_chunks, 2, part, width), F32),
             pltpu.VMEM((n_chunks, 2, part, width), BF16),
             pltpu.VMEM((n_chunks, 2, part, width), BF16),
+            pltpu.SemaphoreType.DMA((n_tp - 1,)),
+            pltpu.SemaphoreType.DMA((n_tp - 1,)),
             pltpu.SemaphoreType.DMA((tiles + n_tp,)),
             pltpu.SemaphoreType.DMA((13,)),
             pltpu.SemaphoreType.DMA((13,)),
@@ -329,8 +379,8 @@
             collective_id=0, has_side_effects=True, vmem_limit_bytes=56 * 2**20),
         name="layer",
     )(
-        token_ids.reshape(1, rows), marks.reshape(1, rows), table, norm_gain.reshape(1, model),
-        w_query, w_key, w_value, decay_idx, out_gain.reshape(1, columns), w_out,
+        token_ids.reshape(1, rows), marks.reshape(1, rows), table, norm_gain,
+        w_query, w_key, w_value, decay_idx, out_gain, w_out,
     )
 
 

time: 47.1 us -> 45.1 us (0.958)
  local copies, waits for them, and re-layouts: 4.34 us -> 1.78 us
  Pallas kernels: 42.5 us -> 43.2 us
    reshape x2 -> x0, local copies, waits for them, and re-layouts: 2.56 us -> none  [the longest x1 1.3 us: per_device(): norm_gain.reshape(1, model)]
    pallas_call x1, Pallas kernels: 42.5 us -> 43.2 us  [per_device(): pl.pallas_call(functools.partial(layer, n_ctx, chunk), out_shape=jax.Shap...]
where the time goes in v2:
time: 45.1 us; the launch traced here: 45 us
  Pallas kernels  43.2 us (96%)
  local copies, waits for them, and re-layouts  1.78 us (4%)
    pallas_call x1, Pallas kernels, per_device(): pl.pallas_call(functools.partial(layer, n_ctx, chunk), out_shape=jax.Shap...  43.2 us
    unnamed x1, local copies, waits for them, and re-layouts  1.78 us

profile of v2, /device:TPU:0, one launch (start us, length us, event | category | flops | bytes accessed | tf_op | source)
XLA Modules:
  0.0 45.0 jit_solution(16616237444139097954)
XLA Ops:
  0.0 43.2 %layer.1 = bf16[512,384]{1,0:T(8,128)(2,1)} custom-call(s32[1,512]{1,0:T(1,128)} %bitcast.2, s32[1,512]{1,0:T(1,128)} %bitcast.3, bf16[256,384]{1,0:T(8,128)(2,1)} %table_ref.1, bf16[3072]{0:T(1024)(128)(2,1)} %gain_ref.1, bf16[3072,512]{1,0:T(8,128)(2,1)} %wq_ref.1, bf16[3072,512]{1,0:T(8,128)(2,1)} %wk_ref.1, bf16[3072,512]{1,0:T(8,128)(2,1)} %wv_ref.1, ...), custom_call_target="tpu_custom_call" | custom-call | tf_op jit(solution)/shard_map/layer/pallas_call | solution.py:338
  43.2 1.8 %copy.12 = bf16[512,384]{1,0:T(8,128)(2,1)} copy(bf16[512,384]{1,0:T(8,128)(2,1)} %layer.1) | data formatting | bytes 786432
